TPU v7x, 32 devices: a whole 2x2x4 slice. The times are simulated.
32 devices in a mesh: stream: 8 (over y, x, core), tp: 4 (over z).
Axes of the slice: x: 2, y: 2, z: 4, core: 2. Of those that a mesh axis runs over, the one named last changes fastest.
Arguments:
- tokens: bfloat16 [12288, 3072], P('stream', 'tp'), may hold values from -6 to 6
- qkv_weight: bfloat16 [3072, 3, 2048], P('stream', None, 'tp'), may hold values from -0.109375 to 0.109375
- gate_weight: bfloat16 [3072, 2048], P('stream', 'tp'), may hold values from -0.109375 to 0.109375
- out_weight: bfloat16 [2048, 3072], P('tp', 'stream'), may hold values from -0.125 to 0.125
- log_decay: float32 [32, 12288], P('tp', 'stream'), may hold values from -1 to 0
- states: float32 [96, 32, 64, 64], P('stream', 'tp'), may hold values from -48 to 48
- dest_slot: int32 [96], P('stream'), may hold values from 0 to 95, as said below
- valid: int32 [96], P('stream'), may hold values from 1 to 128
Outputs:
- mixed: bfloat16 [12288, 3072], P('stream', 'tp')
- new_states: float32 [96, 32, 64, 64], P('stream', 'tp')
Inputs may be any that keep to these rules, and one draw needn't show every extreme that they name: dest_slot is a permutation of the streams; of the 12 streams of one device, at most 2 have new positions on any one device, and that many do for some pair of devices.
All inputs are finite; a program needn't handle non-finite values.
Results may differ from a plain program's by a relative error of at most 0.0058.
Values may be sent and summed in bfloat16 or wider, within the bound.
A program may use at most 128 MiB of HBM per device.

v0:
```python
import jax
import jax.numpy as jnp
from jax import lax
from jax.sharding import PartitionSpec as P

HD = 64
WINDOW_LENGTH = 128


def move_states(states, dest_slot):
    streams = states.shape[0]
    node_count = lax.axis_size("stream")
    capacity = (streams + node_count - 1) // node_count
    target = dest_slot // streams
    places = dest_slot % streams
    order = jnp.arange(streams, dtype=jnp.int32)
    earlier = (target[None, :] == target[:, None]) & (order[None, :] < order[:, None])
    ranking = jnp.sum(earlier.astype(jnp.int32), axis=1)
    position = target * capacity + ranking
    tail_shape = states.shape[1:]
    outgoing = (
        jnp.zeros((node_count * capacity,) + tail_shape, jnp.float32).at[position].set(states)
    )
    outgoing = outgoing.reshape((node_count, capacity) + tail_shape)
    labels = jnp.full((node_count * capacity,), streams, jnp.int32).at[position].set(places)
    labels = labels.reshape(node_count, capacity)
    incoming, incoming_labels = (
        lax.all_to_all(outgoing, "stream", split_axis=0, concat_axis=0, tiled=True),
        lax.all_to_all(labels, "stream", split_axis=0, concat_axis=0, tiled=True),
    )
    flat_states = incoming.reshape((node_count * capacity,) + tail_shape)
    flat_labels = incoming_labels.reshape(node_count * capacity)
    placed = jnp.zeros((streams + 1,) + tail_shape, jnp.float32).at[flat_labels].set(flat_states)
    return placed[:streams]


def body(tokens, qkv_weight, gate_weight, out_weight, log_decay, states, dest_slot, valid):
    streams = states.shape[0]
    heads = states.shape[1]
    length = WINDOW_LENGTH
    rows = streams * length
    moved = move_states(states, dest_slot)
    features_all = lax.all_gather(tokens, "tp", axis=1, tiled=True)
    pieces = (
        lax.all_gather(qkv_weight, "stream", axis=0, tiled=True),
        lax.all_gather(gate_weight, "stream", axis=0, tiled=True),
    )
    count = pieces[1].shape[0]
    qkv_part = jnp.dot(
        features_all, pieces[0].reshape(count, -1), preferred_element_type=jnp.float32
    )
    gate_part = jnp.dot(features_all, pieces[1], preferred_element_type=jnp.float32)
    activated = jax.nn.silu(qkv_part).astype(jnp.bfloat16).reshape(streams, length, 3, heads, HD)
    positions = jnp.arange(length, dtype=jnp.int32)
    live = positions[None, :] < valid[:, None]
    live_half = live.astype(jnp.bfloat16)[:, :, None, None]
    live_full = live.astype(jnp.float32)
    query = activated[:, :, 0]
    lookup_vectors = activated[:, :, 1] * live_half
    values = activated[:, :, 2] * live_half
    decay = log_decay.reshape(heads, streams, length).transpose(1, 0, 2) * live_full[:, None, :]
    lower_ones = (positions[:, None] <= positions[None, :]).astype(jnp.float32)
    cumulative = jnp.einsum("shu,ut->sht", decay, lower_ones, precision=lax.Precision.HIGHEST)
    scores = jnp.einsum(
        "sthd,suhd->shtu", query, lookup_vectors, preferred_element_type=jnp.float32
    )
    causal = positions[:, None] >= positions[None, :]
    gap = cumulative[:, :, :, None] - cumulative[:, :, None, :]
    weights = jnp.where(causal, jnp.exp(jnp.minimum(gap, 0.0)), 0.0)
    probs = (scores * weights).astype(jnp.bfloat16)
    intra = jnp.einsum("shtu,suhd->sthd", probs, values, preferred_element_type=jnp.float32)
    query_full = query.astype(jnp.float32)
    carried = jnp.einsum("sthd,shde->sthe", query_full, moved, precision=lax.Precision.HIGHEST)
    carried = carried * jnp.exp(cumulative).transpose(0, 2, 1)[:, :, :, None]
    attended = intra + carried
    final_log = cumulative[:, :, length - 1 :]
    weighted_keys = (
        lookup_vectors.astype(jnp.float32)
        * jnp.exp(final_log - cumulative).transpose(0, 2, 1)[:, :, :, None]
    )
    updated = jnp.exp(final_log)[:, :, :, None] * moved + jnp.einsum(
        "sthd,sthe->shde",
        weighted_keys,
        values.astype(jnp.float32),
        precision=lax.Precision.HIGHEST,
    )
    mean_square = jnp.mean(attended * attended, axis=-1, keepdims=True)
    normed = attended * lax.rsqrt(mean_square + 1e-05)
    gates = jax.nn.sigmoid(gate_part).reshape(streams, length, heads, HD)
    hidden = (
        (normed * gates * live_full[:, :, None, None])
        .astype(jnp.bfloat16)
        .reshape(rows, heads * HD)
    )
    all_heads = lax.all_gather(hidden, "tp", axis=1, tiled=True)
    group_rows = lax.all_gather(out_weight, "stream", axis=1, tiled=True)
    full_rows = lax.all_to_all(group_rows, "tp", split_axis=1, concat_axis=0, tiled=True)
    mixed = jnp.dot(all_heads, full_rows, preferred_element_type=jnp.float32).astype(jnp.bfloat16)
    return (mixed, updated)


def solution(mesh):
    return jax.shard_map(
        body,
        mesh=mesh,
        in_specs=(
            P("stream", "tp"),
            P("stream", None, "tp"),
            P("stream", "tp"),
            P("tp", "stream"),
            P("tp", "stream"),
            P("stream", "tp", None, None),
            P("stream"),
            P("stream"),
        ),
        out_specs=(P("stream", "tp"), P("stream", "tp", None, None)),
        check_vma=False,
    )
```

profile of v0, /device:TPU:0, one launch (start us, length us, event | category | flops | bytes accessed | tf_op | source)
XLA Modules:
  0.0 544.0 jit_solution(4965468959096347591)
XLA Ops:
  11.7 5.2 all-to-all-start
  16.8 2.6 broadcast_in_dim.13
  19.4 6.5 %scatter_fusion = f32[16,8,64,64]{3,2,1,0:T(8,128)} fusion(f32[16,8,64,64]{3,2,1,0:T(8,128)} %broadcast_in_dim.13, s32[12]{0:T(128)S(1)} %compare_select_fusion.1, f32[12,8,64,64]{3,2,1,0:T(8,128)S(1)} %copy-done.3), kind=kCustom, calls=%fused_computation.1 | custom fusion | bytes 4718640 | tf_op jit(solution)/shard_map/scatter | solution.py:22
  25.9 7.2 %reshape.182 = f32[8,1,65536]{2,1,0:T(1,128)} reshape(f32[8,2,8,64,64]{4,3,2,1,0:T(8,128)} %bitcast.69) | data formatting | bytes 4194304
  33.1 4.2 all-to-all-start.1
  42.8 24.0 %all-to-all-done.1 = f32[8,1,65536]{2,1,0:T(1,128)S(1)} async-done(((f32[8,1,65536]{2,1,0:T(1,128)}), f32[8,1,65536]{2,1,0:T(1,128)S(1)}, u32[]{:S(2)}, u32[]{:S(2)}) %all-to-all-start.1) | async-done | bytes 2097184 | tf_op jit(solution)/shard_map/all_to_all | solution.py:28
  68.5 7.1 %reduce.4 = f32[8,65536]{1,0:T(8,128)S(1)} reduce(f32[8,1,65536]{2,1,0:T(1,128)} %copy-done.1, f32[]{:T(128)} %broadcast.115), dimensions={1}, to_apply=%all_to_all.25.reduce_sub_computation | reduce | bytes 4194308 | tf_op jit(solution)/shard_map/all_to_all | solution.py:28
  75.6 3.7 reshape.183
  79.8 4.8 scatter_fusion.1
  84.6 137.1 %all-gather.6.cloned.1.call-done = bf16[1536,3072]{1,0:T(8,128)(2,1)} async-done(((bf16[1536,768]{1,0:T(8,128)(2,1)}), bf16[1536,3072]{1,0:T(8,128)(2,1)}) %all-gather.6.cloned.1.call-update) | async-done | bytes 9437200 | tf_op jit(solution)/shard_map/all_gather | solution.py:43
  221.7 10.8 %fusion.2 = f32[1536,512]{1,0:T(8,128)} fusion(bf16[1536,3072]{1,0:T(8,128)(2,1)} %all-gather.6.cloned.1.call-done, bf16[3072,512]{1,0:T(8,128)(2,1)} %all-gather.10.cloned.1.call-done), kind=kOutput, calls=%fused_computation.10 | convolution fusion | flops 4834197504 | bytes 15728640 | tf_op jit(solution)/shard_map/dot_general | solution.py:52
  232.5 5.7 %reshape.170 = f32[12,128,8,64]{3,2,1,0:T(8,128)} reshape(f32[1536,512]{1,0:T(8,128)} %fusion.2) | data formatting | bytes 6291456 | tf_op jit(solution)/shard_map/reshape | solution.py:89
  238.1 6.1 %copy.106 = f32[12,128,8,64]{1,3,2,0:T(8,128)} copy(f32[12,128,8,64]{3,2,1,0:T(8,128)} %reshape.170) | data formatting | bytes 6291456 | tf_op jit(solution)/shard_map/reshape | solution.py:89
  244.2 38.1 %all-gather.8.cloned.1.call-done = bf16[3072,3,512]{0,2,1:T(8,128)(2,1)} async-done(((bf16[384,3,512]{0,2,1:T(8,128)(2,1)}), bf16[3072,3,512]{0,2,1:T(8,128)(2,1)}) %all-gather.8.cloned.1.call-update) | async-done | bytes 9437200 | tf_op jit(solution)/shard_map/all_gather | solution.py:45
  282.4 22.6 %multiply_convert_fusion = bf16[1536,1536]{1,0:T(8,128)(2,1)} fusion(bf16[1536,3072]{1,0:T(8,128)(2,1)} %all-gather.6.cloned.1.call-done, bf16[3072,1536]{0,1:T(8,128)(2,1)} %bitcast.76), kind=kOutput, calls=%fused_computation.3 | convolution fusion | flops 14507311104 | bytes 23592960 | tf_op jit(solution)/shard_map/dot_general | solution.py:49
  304.9 6.7 %copy.99 = bf16[1536,1536]{0,1:T(8,128)(2,1)} copy(bf16[1536,1536]{1,0:T(8,128)(2,1)} %multiply_convert_fusion) | data formatting | bytes 9437184 | tf_op jit(solution)/shard_map/convert_element_type | solution.py:53
  311.7 9.5 %reshape.136 = bf16[12,128,3,8,64]{1,0,4,3,2:T(8,128)(2,1)} reshape(bf16[1536,1536]{0,1:T(8,128)(2,1)} %copy.99) | data formatting | bytes 9437184 | tf_op jit(solution)/shard_map/reshape | solution.py:53
  321.2 3.3 slice.21
  324.4 3.1 fusion.14
  327.6 4.9 convert_multiply_fusion
  332.4 9.0 %fusion.3 = f32[12,8,64,128]{3,2,1,0:T(8,128)} fusion(f32[12,8,128]{2,1,0:T(8,128)S(1)} %fusion.22, pred[128,128]{1,0:T(8,128)(4,1)} %iota_compare_fusion.1, bf16[12,128,8,64]{1,0,3,2:T(8,128)(2,1)} %get-tuple-element.15, bf16[12,128,1,8,64]{1,0,4,3,2:T(8,128)(2,1)} %slice.21, bf16[12,128,8,64]{1,0,3,2:T(8,128)(2,1)} %fusion.14), kind=kOutput, calls=%fused_computation.11 | convolution fusion | flops 410517504 | bytes 7929856 | tf_op jit(solution)/shard_map/shtu,suhd->sthd/dot_general | solution.py:71
  341.4 5.3 multiply_reduce_fusion
  348.7 1.6 copy.144
  350.3 4.8 all-to-all-start.2
  355.4 1.9 slice.24
  357.3 2.8 copy.122
  360.1 146.4 %all-to-all-done.2 = bf16[512,4,768]{0,2,1:T(8,128)(2,1)} async-done(((bf16[512,4,768]{0,2,1:T(8,128)(2,1)}), bf16[512,4,768]{0,2,1:T(8,128)(2,1)}, u32[]{:S(2)}, u32[]{:S(2)}) %all-to-all-start.2) | async-done | bytes 3145760 | tf_op jit(solution)/shard_map/all_to_all | solution.py:97
  506.5 4.6 copy.109
  511.1 8.4 %multiply_add_fusion = f32[12,8,64,64]{2,3,1,0:T(8,128)} fusion(f32[12,8,64,64]{2,3,1,0:T(8,128)S(1)} %copy.122, f32[12,128,8,64]{1,0,3,2:T(8,128)} %get-tuple-element.14, f32[12,8]{1,0:T(8,128)S(1)} %copy.111, bf16[12,128,8,64]{1,0,3,2:T(8,128)(2,1)} %fusion.14), kind=kOutput, calls=%fused_computation.16 | convolution fusion | flops 604766208 | bytes 7864704 | tf_op jit(solution)/shard_map/sthd,sthe->shde/dot_general | solution.py:81
  519.6 3.7 copy.117
  523.3 4.8 all-gather.12.cloned.1.call-done
  528.0 9.2 %convolution_convert_fusion = bf16[1536,768]{1,0:T(8,128)(2,1)} fusion(bf16[1536,2048]{0,1:T(8,128)(2,1)} %all-gather.12.cloned.1.call-done, bf16[2048,768]{1,0:T(8,128)(2,1)S(1)} %bitcast.74), kind=kOutput, calls=%fused_computation.6 | convolution fusion | flops 4833017856 | bytes 11796480 | tf_op jit(solution)/shard_map/dot_general | solution.py:98
  (65 shorter events, 14.3 us)
Async XLA Ops:
  7.2 1.6 copy-start.4
  7.2 3.0 copy-start.12
  7.2 77.4 %all-gather.10.cloned.1.call-start = ((), (), s32[]{:S(2)}) async-start(), calls=%async_computation.5 | async-start | bytes 3538944 | tf_op jit(solution)/shard_map/all_gather | solution.py:46
  7.9 213.8 %all-gather.6.cloned.1.call-start = ((), (), s32[]{:S(2)}) async-start(), calls=%async_computation.3 | async-start | bytes 11796480 | tf_op jit(solution)/shard_map/all_gather | solution.py:43
  8.7 273.7 %all-gather.8.cloned.1.call-start = ((), (), s32[]{:S(2)}) async-start(), calls=%async_computation.4 | async-start | bytes 10616832 | tf_op jit(solution)/shard_map/all_gather | solution.py:45
  10.1 9.3 %copy-start.3 = (f32[12,8,64,64]{3,2,1,0:T(8,128)S(1)}, f32[12,8,64,64]{3,2,1,0:T(8,128)}, u32[]{:S(2)}) copy-start(f32[12,8,64,64]{3,2,1,0:T(8,128)} %param.13) | copy-start | bytes 4718596
  11.7 21.5 %all-to-all-start = ((s32[8,1,2]{2,1,0:T(1,128)}), s32[8,1,2]{2,1,0:T(1,128)S(1)}, u32[]{:S(2)}, u32[]{:S(2)}) async-start(s32[8,1,2]{2,1,0:T(1,128)} %bitcast.8), calls=%async_computation | async-start | bytes 8192 | tf_op jit(solution)/shard_map/all_to_all | solution.py:29
  33.1 4.2 copy-start.5
  33.1 5.3 copy-start.11
  33.1 5.9 %copy-start.9 = (f32[8,1536]{1,0:T(8,128)S(1)}, f32[8,1536]{1,0:T(8,128)}, u32[]{:S(2)}) copy-start(f32[8,1536]{1,0:T(8,128)} %param.12) | copy-start | bytes 147460
  33.1 33.6 %all-to-all-start.1 = ((f32[8,1,65536]{2,1,0:T(1,128)}), f32[8,1,65536]{2,1,0:T(1,128)S(1)}, u32[]{:S(2)}, u32[]{:S(2)}) async-start(f32[8,1,65536]{2,1,0:T(1,128)} %reshape.182), calls=%async_computation.1 | async-start | bytes 4194304 | tf_op jit(solution)/shard_map/all_to_all | solution.py:28
  37.3 313.0 %all-gather.14.cloned.1.call-start = ((), (), s32[]{:S(2)}) async-start(), calls=%async_computation.7 | async-start | bytes 3538944 | tf_op jit(solution)/shard_map/all_gather | solution.py:96
  38.3 489.7 %all-gather.12.cloned.1.call-start = ((), (), s32[]{:S(2)}) async-start(), calls=%async_computation.6 | async-start | bytes 7864320 | tf_op jit(solution)/shard_map/all_gather | solution.py:95
  39.1 0.6 copy-start.7
  66.7 1.3 copy-start.1
  321.2 3.3 copy-start.10
  324.4 3.1 copy-start.6
  341.4 5.4 copy-start
  341.4 5.4 copy-start.8
  350.3 156.2 %all-to-all-start.2 = ((bf16[512,4,768]{0,2,1:T(8,128)(2,1)}), bf16[512,4,768]{0,2,1:T(8,128)(2,1)}, u32[]{:S(2)}, u32[]{:S(2)}) async-start(bf16[512,4,768]{0,2,1:T(8,128)(2,1)} %bitcast.73), calls=%async_computation.2 | async-start | bytes 6291456 | tf_op jit(solution)/shard_map/all_to_all | solution.py:97
  519.6 8.5 %copy-start.2 = (bf16[4,512,768]{2,1,0:T(8,128)(2,1)S(1)}, bf16[4,512,768]{2,1,0:T(8,128)(2,1)}, u32[]{:S(2)}) copy-start(bf16[4,512,768]{2,1,0:T(8,128)(2,1)} %copy.109) | copy-start | bytes 9437188
Sparse Core Ops, SparseCore 0:
  9.9 37.7 all-gather.9
  49.3 172.3 all-gather.5
  223.6 58.7 all-gather.7
  284.1 32.3 all-gather.13
  350.4 177.5 all-gather.11
where the time goes:
time: 552 us; the launch traced here: 544 us
  waiting for transfers between devices  352 us (64%)
  local copies, waits for them, and re-layouts  79.4 us (14%)
  matrix products  65.5 us (12%)
  other arithmetic  18.7 us (3%)
  starting transfers between devices  14.4 us (3%)
  between operations  14.2 us (3%)
    all_to_all x1, waiting for transfers between devices, body(): lax.all_to_all(group_rows, 'tp', split_axis=1, concat_axis=0, tiled=True)  146 us
    all_gather x1, waiting for transfers between devices, body(): features_all = lax.all_gather(tokens, 'tp', axis=1, tiled=True)  137 us
    all_gather x1, waiting for transfers between devices, body(): lax.all_gather(qkv_weight, 'stream', axis=0, tiled=True)  38.1 us
    unnamed x35, local copies, waits for them, and re-layouts  24.8 us
    all_to_all x1, waiting for transfers between devices, move_states(): lax.all_to_all(outgoing, 'stream', split_axis=0, concat_axis=0, tiled=True)  24 us
    dot_general x1, matrix products, body(): jnp.dot(features_all, pieces[0].reshape(count, -1), preferred_element_typ...  22.6 us
    reshape x2, local copies, waits for them, and re-layouts, body(): gates = jax.nn.sigmoid(gate_part).reshape(streams, length, heads, HD)  11.8 us
  transfers between devices with their start and end apart: 8, of which 5 were waited for; matrix products, arithmetic and copies ran while one was open for 28% of the time, Pallas kernels for 0%

commit v1 on v0

--- a/solution.py
+++ b/solution.py
@@ -40,7 +40,12 @@
     length = WINDOW_LENGTH
     rows = streams * length
     moved = move_states(states, dest_slot)
-    features_all = lax.all_gather(tokens, "tp", axis=1, tiled=True)
+    ring = [tokens]
+    for hop in range(3):
+        ring.append(lax.ppermute(ring[-1], "tp", [(dev, (dev + 1) % 4) for dev in range(4)]))
+    features_all = jnp.roll(
+        jnp.concatenate(ring[::-1], axis=1), (lax.axis_index("tp") + 1) * ring[0].shape[1], axis=1
+    )
     pieces = (
         lax.all_gather(qkv_weight, "stream", axis=0, tiled=True),
         lax.all_gather(gate_weight, "stream", axis=0, tiled=True),

time: 552 us -> 507 us (0.918)
  waiting for transfers between devices: 352 us -> 281 us
  local copies, waits for them, and re-layouts: 79.4 us -> 102 us
    all_gather x1 -> x0, waiting for transfers between devices: 137 us -> none  [body(): features_all = lax.all_gather(tokens, 'tp', axis=1, tiled=True)]
    ppermute x0 -> x3, waiting for transfers between devices: none -> 108 us  [body(): lax.ppermute(ring[-1], 'tp', [(dev, (dev + 1) % 4) for dev in range(4)])]
    all_gather x1, waiting for transfers between devices: 38.1 us -> 0.01 us  [body(): lax.all_gather(qkv_weight, 'stream', axis=0, tiled=True)]
    unnamed x35 -> x48, local copies, waits for them, and re-layouts: 24.8 us -> 46.3 us
  transfers between devices with their start and end apart: 8 -> 10, of which waited for: 5 -> 5; matrix products, arithmetic and copies ran while one was open for 28% -> 34% of each run, Pallas kernels for 0% -> 0%
where the time goes in v1:
time: 507 us; the launch traced here: 497 us
  waiting for transfers between devices  281 us (55%)
  local copies, waits for them, and re-layouts  102 us (20%)
  matrix products  64 us (13%)
  other arithmetic  18.8 us (4%)
  starting transfers between devices  16.3 us (3%)
  between operations  14.2 us (3%)
    all_to_all x1, waiting for transfers between devices, body(): lax.all_to_all(group_rows, 'tp', split_axis=1, concat_axis=0, tiled=True)  143 us
    ppermute x3, waiting for transfers between devices, body(): lax.ppermute(ring[-1], 'tp', [(dev, (dev + 1) % 4) for dev in range(4)])  108 us
    unnamed x48, local copies, waits for them, and re-layouts  46.3 us
    all_to_all x1, waiting for transfers between devices, move_states(): lax.all_to_all(outgoing, 'stream', split_axis=0, concat_axis=0, tiled=True)  25.5 us
    dot_general x1, matrix products, body(): jnp.dot(features_all, pieces[0].reshape(count, -1), preferred_element_typ...  21.9 us
    reshape x2, local copies, waits for them, and re-layouts, body(): gates = jax.nn.sigmoid(gate_part).reshape(streams, length, heads, HD)  11.7 us
    dot_general x1, matrix products, body(): jnp.dot(features_all, pieces[1], preferred_element_type=jnp.float32)  10.3 us
  transfers between devices with their start and end apart: 10, of which 5 were waited for; matrix products, arithmetic and copies ran while one was open for 34% of the time, Pallas kernels for 0%

profile of v1, /device:TPU:0, one launch (start us, length us, event | category | flops | bytes accessed | tf_op | source)
XLA Modules:
  0.0 496.9 jit_solution(10862066982848961274)
XLA Ops:
  13.5 53.3 %collective-permute-done = bf16[1536,768]{1,0:T(8,128)(2,1)S(1)} collective-permute-done((bf16[1536,768]{1,0:T(8,128)(2,1)S(1)}, bf16[1536,768]{1,0:T(8,128)(2,1)S(1)}, u32[]{:S(2)}, u32[]{:S(2)}) %collective-permute-start) | collective-permute-done | bytes 2359328 | tf_op jit(solution)/shard_map/ppermute | solution.py:45
  68.1 54.3 %collective-permute-done.1 = bf16[1536,768]{1,0:T(8,128)(2,1)} collective-permute-done((bf16[1536,768]{1,0:T(8,128)(2,1)S(1)}, bf16[1536,768]{1,0:T(8,128)(2,1)}, u32[]{:S(2)}, u32[]{:S(2)}) %collective-permute-start.1) | collective-permute-done | bytes 2359328 | tf_op jit(solution)/shard_map/ppermute | solution.py:45
  124.0 3.5 all-to-all-start
  129.9 6.3 %scatter_fusion = f32[16,8,64,64]{3,2,1,0:T(8,128)} fusion(f32[16,8,64,64]{3,2,1,0:T(8,128)} %broadcast_in_dim.13, s32[12]{0:T(128)S(1)} %compare_select_fusion.1, f32[12,8,64,64]{3,2,1,0:T(8,128)S(1)} %copy-done.7), kind=kCustom, calls=%fused_computation.1 | custom fusion | bytes 4718640 | tf_op jit(solution)/shard_map/scatter | solution.py:22
  136.2 7.2 %reshape.182 = f32[8,1,65536]{2,1,0:T(1,128)} reshape(f32[8,2,8,64,64]{4,3,2,1,0:T(8,128)} %bitcast.64) | data formatting | bytes 4194304
  143.4 4.3 all-to-all-start.1
  153.1 25.5 %all-to-all-done.1 = f32[8,1,65536]{2,1,0:T(1,128)S(1)} async-done(((f32[8,1,65536]{2,1,0:T(1,128)}), f32[8,1,65536]{2,1,0:T(1,128)S(1)}, u32[]{:S(2)}, u32[]{:S(2)}) %all-to-all-start.1) | async-done | bytes 2097184 | tf_op jit(solution)/shard_map/all_to_all | solution.py:28
  180.4 7.3 %reduce.4 = f32[8,65536]{1,0:T(8,128)S(1)} reduce(f32[8,1,65536]{2,1,0:T(1,128)} %copy-done.5, f32[]{:T(128)} %broadcast.119), dimensions={1}, to_apply=%all_to_all.25.reduce_sub_computation | reduce | bytes 4194308 | tf_op jit(solution)/shard_map/all_to_all | solution.py:28
  187.7 3.6 reshape.183
  191.7 5.1 %scatter_fusion.1 = f32[13,8,64,64]{3,2,1,0:T(8,128)S(1)} fusion(f32[13,8,64,64]{3,2,1,0:T(8,128)S(1)} %broadcast_in_dim.11, s32[16]{0:T(128)} %fusion.40, f32[16,8,64,64]{3,2,1,0:T(8,128)} %bitcast.65), kind=kCustom, calls=%fused_computation.2 | custom fusion | bytes 6291520 | tf_op jit(solution)/shard_map/scatter | solution.py:33
  196.8 3.4 constant_dynamic-update-slice_fusion.7
  200.2 3.5 constant_dynamic-update-slice_fusion.6
  207.8 3.3 constant_dynamic-update-slice_fusion.3
  211.1 3.2 constant_dynamic-update-slice_fusion.2
  217.6 10.3 %add_divide_fusion = f32[1536,512]{1,0:T(8,128)} fusion(bf16[3072,512]{1,0:T(8,128)(2,1)} %all-gather.7.cloned.1.call-done, bf16[1536,6144]{1,0:T(8,128)(2,1)} %constant_dynamic-update-slice_fusion, s32[]{:T(128)S(6)} %select_n.43), kind=kOutput, calls=%fused_computation.20 | convolution fusion | flops 4834197504 | bytes 15728644 | tf_op jit(solution)/shard_map/dot_general | solution.py:57
  227.9 5.6 %reshape.170 = f32[12,128,8,64]{3,2,1,0:T(8,128)} reshape(f32[1536,512]{1,0:T(8,128)} %add_divide_fusion) | data formatting | bytes 6291456 | tf_op jit(solution)/shard_map/reshape | solution.py:94
  233.5 6.1 %copy.106 = f32[12,128,8,64]{1,3,2,0:T(8,128)} copy(f32[12,128,8,64]{3,2,1,0:T(8,128)} %reshape.170) | data formatting | bytes 6291456 | tf_op jit(solution)/shard_map/reshape | solution.py:94
  239.6 21.9 %multiply_convert_fusion = bf16[1536,1536]{1,0:T(8,128)(2,1)} fusion(bf16[3072,1536]{0,1:T(8,128)(2,1)} %bitcast.71, bf16[1536,6144]{1,0:T(8,128)(2,1)} %constant_dynamic-update-slice_fusion, s32[]{:T(128)S(6)} %select_n.43), kind=kOutput, calls=%fused_computation.3 | convolution fusion | flops 14507311104 | bytes 23592964 | tf_op jit(solution)/shard_map/dot_general | solution.py:54
  261.6 6.7 %copy.99 = bf16[1536,1536]{0,1:T(8,128)(2,1)} copy(bf16[1536,1536]{1,0:T(8,128)(2,1)} %multiply_convert_fusion) | data formatting | bytes 9437184 | tf_op jit(solution)/shard_map/convert_element_type | solution.py:58
  268.2 9.4 %reshape.136 = bf16[12,128,3,8,64]{1,0,4,3,2:T(8,128)(2,1)} reshape(bf16[1536,1536]{0,1:T(8,128)(2,1)} %copy.99) | data formatting | bytes 9437184 | tf_op jit(solution)/shard_map/reshape | solution.py:58
  277.7 3.3 slice.21
  280.9 3.1 fusion.25
  284.0 4.9 convert_multiply_fusion
  288.9 8.7 %fusion.12 = f32[12,8,64,128]{3,2,1,0:T(8,128)} fusion(f32[12,8,128]{2,1,0:T(8,128)S(1)} %fusion.33, pred[128,128]{1,0:T(8,128)(4,1)} %iota_compare_fusion.1, bf16[12,128,8,64]{1,0,3,2:T(8,128)(2,1)} %get-tuple-element.15, bf16[12,128,1,8,64]{1,0,4,3,2:T(8,128)(2,1)} %slice.21, bf16[12,128,8,64]{1,0,3,2:T(8,128)(2,1)} %fusion.25), kind=kOutput, calls=%fused_computation.13 | convolution fusion | flops 410517504 | bytes 7929856 | tf_op jit(solution)/shard_map/shtu,suhd->sthd/dot_general | solution.py:76
  297.6 5.3 %multiply_reduce_fusion = (f32[12,128,8]{1,2,0:T(8,128)S(1)}, f32[12,128,8,64]{1,3,2,0:T(8,128)S(1)}) fusion(f32[12,128,8]{1,2,0:T(8,128)S(1)} %get-tuple-element.16, f32[13,8,64,64]{3,2,1,0:T(8,128)S(1)} %scatter_fusion.1, bf16[12,128,1,8,64]{1,0,4,3,2:T(8,128)(2,1)} %slice.21, f32[12,8,64,128]{3,2,1,0:T(8,128)} %fusion.12), kind=kOutput, calls=%fused_computation.21 | convolution fusion | flops 607113216 | bytes 9666560 | tf_op jit(solution)/shard_map/sthd,shde->sthe/dot_general | solution.py:78
  306.6 5.3 %all-to-all-start.2 = ((bf16[512,4,768]{0,2,1:T(8,128)(2,1)}), bf16[512,4,768]{0,2,1:T(8,128)(2,1)}, u32[]{:S(2)}, u32[]{:S(2)}) async-start(bf16[512,4,768]{0,2,1:T(8,128)(2,1)} %bitcast.68), calls=%async_computation.2 | async-start | bytes 6291456 | tf_op jit(solution)/shard_map/all_to_all | solution.py:102
  316.7 142.9 %all-to-all-done.2 = bf16[512,4,768]{0,2,1:T(8,128)(2,1)} async-done(((bf16[512,4,768]{0,2,1:T(8,128)(2,1)}), bf16[512,4,768]{0,2,1:T(8,128)(2,1)}, u32[]{:S(2)}, u32[]{:S(2)}) %all-to-all-start.2) | async-done | bytes 3145760 | tf_op jit(solution)/shard_map/all_to_all | solution.py:102
  459.6 4.7 copy.109
  464.3 8.4 %multiply_add_fusion = f32[12,8,64,64]{2,3,1,0:T(8,128)} fusion(f32[12,8,64,64]{2,3,1,0:T(8,128)S(1)} %copy.122, f32[12,128,8,64]{1,0,3,2:T(8,128)} %get-tuple-element.14, f32[12,8]{1,0:T(8,128)S(1)} %copy.111, bf16[12,128,8,64]{1,0,3,2:T(8,128)(2,1)} %fusion.25), kind=kOutput, calls=%fused_computation.18 | convolution fusion | flops 604766208 | bytes 7864704 | tf_op jit(solution)/shard_map/sthd,sthe->shde/dot_general | solution.py:86
  472.7 3.7 copy.117
  476.4 4.5 all-gather.9.cloned.1.call-done
  480.9 9.2 %convolution_convert_fusion = bf16[1536,768]{1,0:T(8,128)(2,1)} fusion(bf16[1536,2048]{0,1:T(8,128)(2,1)} %all-gather.9.cloned.1.call-done, bf16[2048,768]{1,0:T(8,128)(2,1)S(1)} %bitcast.69), kind=kOutput, calls=%fused_computation.10 | convolution fusion | flops 4833017856 | bytes 11796480 | tf_op jit(solution)/shard_map/dot_general | solution.py:103
  (82 shorter events, 34.9 us)
Async XLA Ops:
  7.2 3.2 copy-start.1
  7.2 115.3 %copy-start.15 = (s32[12]{0:T(128)S(1)}, s32[12]{0:T(128)}, u32[]{:S(2)}) copy-start(s32[12]{0:T(128)} %param.14) | copy-start | bytes 148
  7.2 210.5 %all-gather.7.cloned.1.call-start = ((), (), s32[]{:S(2)}) async-start(), calls=%async_computation.4 | async-start | bytes 3538944 | tf_op jit(solution)/shard_map/all_gather | solution.py:51
  7.9 231.7 %all-gather.5.cloned.1.call-start = ((), (), s32[]{:S(2)}) async-start(), calls=%async_computation.3 | async-start | bytes 10616832 | tf_op jit(solution)/shard_map/all_gather | solution.py:50
  10.4 56.3 %collective-permute-start = (bf16[1536,768]{1,0:T(8,128)(2,1)S(1)}, bf16[1536,768]{1,0:T(8,128)(2,1)S(1)}, u32[]{:S(2)}, u32[]{:S(2)}) collective-permute-start(bf16[1536,768]{1,0:T(8,128)(2,1)S(1)} %copy-done.1), channel_id=1, source_target_pairs={{0,1},{1,2},{2,3},{3,0},{4,5},{5,6},{6,7},{7,4},{8,9},{9,10},{10,1... | collective-permute-start | bytes 7077896 | tf_op jit(solution)/shard_map/ppermute | solution.py:45
  66.7 1.4 copy-start.3
  68.1 61.8 %copy-start.7 = (f32[12,8,64,64]{3,2,1,0:T(8,128)S(1)}, f32[12,8,64,64]{3,2,1,0:T(8,128)}, u32[]{:S(2)}) copy-start(f32[12,8,64,64]{3,2,1,0:T(8,128)} %param.13) | copy-start | bytes 4718596
  68.1 54.3 %collective-permute-start.1 = (bf16[1536,768]{1,0:T(8,128)(2,1)S(1)}, bf16[1536,768]{1,0:T(8,128)(2,1)}, u32[]{:S(2)}, u32[]{:S(2)}) collective-permute-start(bf16[1536,768]{1,0:T(8,128)(2,1)S(1)} %collective-permute-done), channel_id=1, source_target_pairs={{0,1},{1,2},{2,3},{3,0},{4,5},{5,6},{6,7},{7,4},{8,9},{9,10},{10,1... | collective-permute-start | bytes 7077896 | tf_op jit(solution)/shard_map/ppermute | solution.py:45
  122.5 74.3 %collective-permute-start.2 = (bf16[1536,768]{1,0:T(8,128)(2,1)}, bf16[1536,768]{1,0:T(8,128)(2,1)}, u32[]{:S(2)}, u32[]{:S(2)}) collective-permute-start(bf16[1536,768]{1,0:T(8,128)(2,1)} %collective-permute-done.1), channel_id=1, source_target_pairs={{0,1},{1,2},{2,3},{3,0},{4,5},{5,6},{6,7},{7,4},{8,9},{9,10},{10,1... | collective-permute-start | bytes 7077896 | tf_op jit(solution)/shard_map/ppermute | solution.py:45
  124.0 19.4 %all-to-all-start = ((s32[8,1,2]{2,1,0:T(1,128)}), s32[8,1,2]{2,1,0:T(1,128)S(1)}, u32[]{:S(2)}, u32[]{:S(2)}) async-start(s32[8,1,2]{2,1,0:T(1,128)} %bitcast.8), calls=%async_computation | async-start | bytes 8192 | tf_op jit(solution)/shard_map/all_to_all | solution.py:29
  143.4 4.4 copy-start.8
  143.4 5.4 %copy-start.14 = (s32[12]{0:T(128)S(1)}, s32[12]{0:T(128)}, u32[]{:S(2)}) copy-start(s32[12]{0:T(128)} %param.15) | copy-start | bytes 148
  143.4 6.1 %copy-start.12 = (f32[8,1536]{1,0:T(8,128)S(1)}, f32[8,1536]{1,0:T(8,128)}, u32[]{:S(2)}) copy-start(f32[8,1536]{1,0:T(8,128)} %param.12) | copy-start | bytes 147460
  143.4 35.2 %all-to-all-start.1 = ((f32[8,1,65536]{2,1,0:T(1,128)}), f32[8,1,65536]{2,1,0:T(1,128)S(1)}, u32[]{:S(2)}, u32[]{:S(2)}) async-start(f32[8,1,65536]{2,1,0:T(1,128)} %reshape.182), calls=%async_computation.1 | async-start | bytes 4194304 | tf_op jit(solution)/shard_map/all_to_all | solution.py:28
  147.7 158.8 %all-gather.11.cloned.1.call-start = ((), (), s32[]{:S(2)}) async-start(), calls=%async_computation.6 | async-start | bytes 3538944 | tf_op jit(solution)/shard_map/all_gather | solution.py:101
  148.8 332.2 %all-gather.9.cloned.1.call-start = ((), (), s32[]{:S(2)}) async-start(), calls=%async_computation.5 | async-start | bytes 7864320 | tf_op jit(solution)/shard_map/all_gather | solution.py:100
  149.5 0.6 copy-start.10
  178.6 1.3 copy-start.5
  200.2 3.5 copy-start.4
  203.7 2.5 copy-start.2
  277.7 3.3 copy-start.13
  280.9 3.1 copy-start.9
  297.6 5.4 %copy-start = (f32[12,128,8,64]{1,3,2,0:T(8,128)S(1)}, f32[12,128,8,64]{1,3,2,0:T(8,128)}, u32[]{:S(2)}) copy-start(f32[12,128,8,64]{1,3,2,0:T(8,128)} %copy.106) | copy-start | bytes 9437188
  297.6 5.4 %copy-start.11 = (f32[12,128]{1,0:T(8,128)S(1)}, f32[12,128]{1,0:T(8,128)}, u32[]{:S(2)}) copy-start(f32[12,128]{1,0:T(8,128)} %copy-done.10) | copy-start | bytes 18436
  306.6 153.1 %all-to-all-start.2 = ((bf16[512,4,768]{0,2,1:T(8,128)(2,1)}), bf16[512,4,768]{0,2,1:T(8,128)(2,1)}, u32[]{:S(2)}, u32[]{:S(2)}) async-start(bf16[512,4,768]{0,2,1:T(8,128)(2,1)} %bitcast.68), calls=%async_computation.2 | async-start | bytes 6291456 | tf_op jit(solution)/shard_map/all_to_all | solution.py:102
  472.7 8.2 %copy-start.6 = (bf16[4,512,768]{2,1,0:T(8,128)(2,1)S(1)}, bf16[4,512,768]{2,1,0:T(8,128)(2,1)}, u32[]{:S(2)}) copy-start(bf16[4,512,768]{2,1,0:T(8,128)(2,1)} %copy.109) | copy-start | bytes 9437188
Sparse Core Ops, SparseCore 0:
  9.9 35.0 all-gather.6
  46.8 60.5 all-gather.4
  150.5 43.9 all-gather.10
  306.7 174.2 all-gather.8
